TPU v7x, 32 devices: a whole 2x2x4 slice. The times are simulated.
32 devices in a mesh: pts: 8 (over z, y), grp: 4 (over x, core).
Axes of the slice: x: 2, y: 2, z: 4, core: 2. Of those that a mesh axis runs over, the one named last changes fastest.
Arguments:
- coords: float32 [3, 16384], P(None, ('pts', 'grp')), may hold values from 0 to 1, as said below
- observations: float32 [16384], P(('pts', 'grp')), may hold values from -18 to 18
- length_scales: float32 [3], replicated, may hold values from 0.3 to 1
- nugget: float32 [1], replicated, may hold values from 0.05 to 0.3
- fetch_table: int32 [32, 32, 41], P(('pts', 'grp')), may hold values from 0 to 511
- slot_of: int32 [30, 16384], P(None, ('pts', 'grp')), may hold values from 0 to 2847, as said below
Outputs:
- whitened: float32 [16384], P(('pts', 'grp'))
- neg_loglik: float32 [], replicated
Inputs may be any that keep to these rules, and one draw needn't show every extreme that they name: `coords`: the points of the device of tile t and slab s have first coordinate in [t / 8, (t + 1) / 8) and time coordinate in [s / 4, (s + 1) / 4). `slot_of`: the 30 slots of one point are distinct. Slots below 1536 never point before the first tile or after the last one. Only the first 32 points of each device use slots of 1536 or more, and each of those slots is used at most once on its device; on every device some owner's 41 far slots are all used.
All inputs are finite; a program needn't handle non-finite values.
Results may differ from a plain program's by a relative error of at most 0.0003.
Values sent between devices are 32-bit elements; how exact they have to be, the bound alone decides.
No kernel may reach another device: no remote copies, remote signals or barrier semaphores. Data moves between devices by JAX's collectives and lax.ppermute only.
A program may use at most 128 MiB of HBM per device.

v0:
```python
import jax
import jax.numpy as jnp
from jax import lax
from jax.sharding import PartitionSpec as P

root_three = 1.7320508075688772
half_log_tau = 0.9189385332046727


def extended(cells, sides, width):
    for axis, dim in sides:
        count = lax.axis_size(axis)
        ends = count - 1
        head = lax.slice_in_dim(cells, 0, width, axis=dim)
        tail = lax.slice_in_dim(cells, cells.shape[dim] - width, cells.shape[dim], axis=dim)
        cells = jnp.concatenate(
            [
                lax.ppermute(tail, axis, [(i, (i + 1) % count) for i in range(ends)]),
                cells,
                lax.ppermute(head, axis, [((i + 1) % count, i) for i in range(ends)]),
            ],
            axis=dim,
        )
    return cells


def covariance(points, inverse_lengths, nugget):
    scaled = points * inverse_lengths[:, None, None]
    gap = scaled[:, :, None, :] - scaled[:, None, :, :]
    distance = jnp.sqrt(jnp.sum(gap * gap, axis=0))
    scaled_distance = root_three * distance
    order = points.shape[1]
    identity = jnp.eye(order, dtype=jnp.float32)[:, :, None]
    return (1.0 + scaled_distance) * jnp.exp(-scaled_distance) + nugget[0] * identity


def eliminate(matrix, values):
    order = matrix.shape[0]
    for step in range(order):
        pivot = jnp.sqrt(matrix[0, 0])
        solved = values[0] / pivot
        if step == order - 1:
            return (solved, pivot)
        column = matrix[1:, 0] / pivot
        matrix = matrix[1:, 1:] - column[:, None, :] * column[None, :, :]
        values = values[1:] - column * solved


def split_three(table):
    upper = table.astype(jnp.bfloat16)
    rest = table - lax.optimization_barrier(upper).astype(jnp.float32)
    middle = rest.astype(jnp.bfloat16)
    lower = (rest - lax.optimization_barrier(middle).astype(jnp.float32)).astype(jnp.bfloat16)
    return jnp.concatenate([upper, middle, lower], axis=0)


def select_slots(table, slot_of):
    pieces = split_three(table)
    width = table.shape[0]
    rows = jnp.arange(table.shape[1], dtype=jnp.int32)[:, None]

    def one_neighbour(indices):
        picker = (rows == indices[None, :]).astype(jnp.bfloat16)
        product = jnp.dot(pieces, picker, preferred_element_type=jnp.float32)
        return product[:width] + (product[width : 2 * width] + product[2 * width :])

    picked = lax.map(one_neighbour, slot_of)
    return jnp.transpose(picked, (1, 0, 2))


def body(coords, observations, length_scales, nugget, fetch_table, slot_of):
    local_count = coords.shape[1]
    owners = fetch_table.shape[1]
    capacity = fetch_table.shape[2]
    my_table = fetch_table[0]
    payload = jnp.concatenate([coords, observations[None, :]], axis=0)
    near = extended(payload, (("pts", 1),), local_count)
    wanted = lax.all_to_all(my_table, ("pts", "grp"), split_axis=0, concat_axis=0, tiled=True)
    served = jnp.take(payload, wanted, axis=1)
    buffer = lax.all_to_all(served, ("pts", "grp"), split_axis=1, concat_axis=1, tiled=True)
    slots = jnp.concatenate([near, buffer.reshape(4, owners * capacity)], axis=1)
    gathered = select_slots(slots, slot_of)
    members = jnp.concatenate([gathered, payload[:, None, :]], axis=1)
    matrix = covariance(members[:3], 1.0 / length_scales, nugget)
    whitened, pivot = eliminate(matrix, members[3])
    partial_value = jnp.sum(2.0 * jnp.log(pivot) + whitened * whitened)
    total = lax.psum(partial_value, ("pts", "grp"))
    everyone = local_count * lax.axis_size("pts") * lax.axis_size("grp")
    neg_loglik = total / (2.0 * everyone) + half_log_tau
    return (whitened, neg_loglik)


def solution(mesh):
    in_specs = (
        P(None, ("pts", "grp")),
        P(("pts", "grp")),
        P(),
        P(),
        P(("pts", "grp"), None, None),
        P(None, ("pts", "grp")),
    )
    out_specs = (P(("pts", "grp")), P())
    return jax.shard_map(body, mesh=mesh, in_specs=in_specs, out_specs=out_specs, check_vma=False)
```

profile of v0, /device:TPU:0, one launch (start us, length us, event | category | flops | bytes accessed | tf_op | source)
XLA Modules:
  0.0 144.1 jit_solution(17001950427612192566)
XLA Ops:
  1.4 1.3 collective-permute-start.1
  2.7 5.5 %collective-permute-start = (f32[4,512]{1,0:T(4,128)S(1)}, f32[4,512]{1,0:T(4,128)S(1)}, u32[]{:S(2)}, u32[]{:S(2)}) collective-permute-start(f32[4,512]{1,0:T(4,128)S(1)} %pad_maximum_fusion.3), channel_id=1, source_target_pairs={{0,4},{4,8},{8,12},{12,16},{16,20},{20,24},{24,28},{1,5},{5,9},{9,... | collective-permute-start | bytes 24584 | tf_op jit(solution)/shard_map/ppermute | solution.py:18
  8.2 6.2 %all-to-all-start = ((s32[32,1,41]{2,1,0:T(1,128)}), s32[32,1,41]{2,1,0:T(1,128)S(1)}, u32[]{:S(2)}, u32[]{:S(2)}) async-start(s32[32,1,41]{2,1,0:T(1,128)} %bitcast.437), calls=%async_computation | async-start | bytes 32768 | tf_op jit(solution)/shard_map/all_to_all | solution.py:78
  16.0 5.6 %all-to-all-done = s32[32,1,41]{2,1,0:T(1,128)S(1)} async-done(((s32[32,1,41]{2,1,0:T(1,128)}), s32[32,1,41]{2,1,0:T(1,128)S(1)}, u32[]{:S(2)}, u32[]{:S(2)}) %all-to-all-start) | async-done | bytes 5280 | tf_op jit(solution)/shard_map/all_to_all | solution.py:78
  21.7 2.6 %gather_fusion = f32[1312,4]{1,0:T(8,128)S(1)} fusion(f32[4,512]{0,1:T(8,128)S(1)} %copy.34, s32[2048]{0:T(1024)S(1)} %pad_clamp_fusion), kind=kCustom, calls=%fused_computation | custom fusion | bytes 47232 | tf_op jit(solution)/shard_map/jit(_take)/gather | solution.py:79
  25.6 2.5 %all-to-all-start.1 = ((f32[32,1,164]{2,1,0:T(1,128)}), f32[32,1,164]{2,1,0:T(1,128)S(1)}, u32[]{:S(2)}, u32[]{:S(2)}) async-start(f32[32,1,164]{2,1,0:T(1,128)} %reshape.1323), calls=%async_computation.1 | async-start | bytes 65536 | tf_op jit(solution)/shard_map/all_to_all | solution.py:80
  28.1 7.2 %all-to-all-done.1 = f32[32,1,164]{2,1,0:T(1,128)S(1)} async-done(((f32[32,1,164]{2,1,0:T(1,128)}), f32[32,1,164]{2,1,0:T(1,128)S(1)}, u32[]{:S(2)}, u32[]{:S(2)}) %all-to-all-start.1) | async-done | bytes 21024 | tf_op jit(solution)/shard_map/all_to_all | solution.py:80
  37.0 56.5 %while.11 = (s32[]{:T(128)}, f32[30,4,512]{2,0,1:T(8,128)S(1)}, s32[30,512]{1,0:T(8,128)}, bf16[12,2848]{1,0:T(8,128)(2,1)S(1)}, s32[]{:T(128)}, /*index=5*/s32[]{:T(128)}) while((s32[]{:T(128)}, f32[30,4,512]{2,0,1:T(8,128)S(1)}, s32[30,512]{1,0:T(8,128)}, bf16[12,2848]{1,0:T(8,128)(2,1)S(1)}, s32[]{:T(128)}, ...), condition=%wide.region_1.2_spmd.clone, body=%wide.region_0.1_spmd.clone.sunk | while | flops 36458496 | bytes 164693 | solution.py:67
  37.7 1.0 fusion.58
  39.6 1.0 fusion.58
  41.5 1.0 fusion.58
  43.4 1.0 fusion.58
  45.3 1.0 fusion.58
  47.2 1.0 fusion.58
  49.0 1.0 fusion.58
  50.9 1.0 fusion.58
  52.8 1.0 fusion.58
  54.7 1.0 fusion.58
  56.6 1.0 fusion.58
  58.4 1.0 fusion.58
  60.3 1.0 fusion.58
  62.2 1.0 fusion.58
  64.1 1.0 fusion.58
  66.0 1.0 fusion.58
  67.9 1.0 fusion.58
  69.7 1.0 fusion.58
  71.6 1.0 fusion.58
  73.5 1.0 fusion.58
  75.4 1.0 fusion.58
  77.3 1.0 fusion.58
  102.7 1.2 add_reduce_fusion
  103.9 38.4 %psum.7 = f32[]{:T(128)} all-reduce(f32[]{:T(128)} %get-tuple-element.48), channel_id=1, replica_groups=mesh['pts'=8,'grp'=4] {'pts','grp'}, use_global_device_ids=true, to_apply=%region_4.5 | all-reduce | flops 1 | bytes 8 | tf_op jit(solution)/shard_map/psum | solution.py:87
  (337 shorter events, 45.4 us)
Async XLA Ops:
  0.6 36.2 %copy-start = (f32[3,512]{1,0:T(4,128)S(1)}, f32[3,512]{1,0:T(4,128)}, u32[]{:S(2)}) copy-start(f32[3,512]{1,0:T(4,128)} %param.8) | copy-start | bytes 18436
  0.6 36.2 %copy-start.1 = (f32[512]{0:T(512)S(1)}, f32[512]{0:T(512)}, u32[]{:S(2)}) copy-start(f32[512]{0:T(512)} %param.9) | copy-start | bytes 6148
  1.4 35.4 %collective-permute-start.1 = (f32[4,512]{1,0:T(4,128)S(1)}, f32[4,512]{1,0:T(4,128)S(1)}, u32[]{:S(2)}, u32[]{:S(2)}) collective-permute-start(f32[4,512]{1,0:T(4,128)S(1)} %pad_maximum_fusion.3), channel_id=1, source_target_pairs={{4,0},{8,4},{12,8},{16,12},{20,16},{24,20},{28,24},{5,1},{9,5},{13... | collective-permute-start | bytes 24584 | tf_op jit(solution)/shard_map/ppermute | solution.py:20
  2.7 34.1 %collective-permute-start = (f32[4,512]{1,0:T(4,128)S(1)}, f32[4,512]{1,0:T(4,128)S(1)}, u32[]{:S(2)}, u32[]{:S(2)}) collective-permute-start(f32[4,512]{1,0:T(4,128)S(1)} %pad_maximum_fusion.3), channel_id=1, source_target_pairs={{0,4},{4,8},{8,12},{12,16},{16,20},{20,24},{24,28},{1,5},{5,9},{9,... | collective-permute-start | bytes 24584 | tf_op jit(solution)/shard_map/ppermute | solution.py:18
  8.2 13.4 %all-to-all-start = ((s32[32,1,41]{2,1,0:T(1,128)}), s32[32,1,41]{2,1,0:T(1,128)S(1)}, u32[]{:S(2)}, u32[]{:S(2)}) async-start(s32[32,1,41]{2,1,0:T(1,128)} %bitcast.437), calls=%async_computation | async-start | bytes 32768 | tf_op jit(solution)/shard_map/all_to_all | solution.py:78
  25.6 9.8 %all-to-all-start.1 = ((f32[32,1,164]{2,1,0:T(1,128)}), f32[32,1,164]{2,1,0:T(1,128)S(1)}, u32[]{:S(2)}, u32[]{:S(2)}) async-start(f32[32,1,164]{2,1,0:T(1,128)} %reshape.1323), calls=%async_computation.1 | async-start | bytes 65536 | tf_op jit(solution)/shard_map/all_to_all | solution.py:80
where the time goes:
time: 147 us; the launch traced here: 144 us
  blocking collectives  38.4 us (26%)
  matrix products  30.6 us (21%)
  local copies, waits for them, and re-layouts  30.2 us (21%)
  starting transfers between devices  15.6 us (11%)
  waiting for transfers between devices  12.8 us (9%)
  other arithmetic  10.8 us (7%)
  between operations  4.68 us (3%)
    psum x1, blocking collectives, body(): total = lax.psum(partial_value, ('pts', 'grp'))  38.4 us
    dot_general x30, matrix products, one_neighbour(): product = jnp.dot(pieces, picker, preferred_element_type=jnp.float32)  30.6 us
    dynamic_slice x30, local copies, waits for them, and re-layouts, select_slots(): picked = lax.map(one_neighbour, slot_of)  21.8 us
    all_to_all x1, waiting for transfers between devices, body(): lax.all_to_all(served, ('pts', 'grp'), split_axis=1, concat_axis=1, tiled...  7.22 us
    all_to_all x1, starting transfers between devices, body(): lax.all_to_all(my_table, ('pts', 'grp'), split_axis=0, concat_axis=0, til...  6.24 us
    all_to_all x1, waiting for transfers between devices, body(): lax.all_to_all(my_table, ('pts', 'grp'), split_axis=0, concat_axis=0, til...  5.63 us
    ppermute x1, starting transfers between devices, extended(): lax.ppermute(tail, axis, [(i, (i + 1) % count) for i in range(ends)])  5.53 us
    sub x29, other arithmetic, eliminate(): matrix = matrix[1:, 1:] - column[:, None, :] * column[None, :, :]  4.26 us
  transfers between devices with their start and end apart: 4, of which 2 were waited for; matrix products, arithmetic and copies ran while one was open for 4% of the time, Pallas kernels for 0%

commit v1 on v0

v1 whole, which is shorter than its diff:
```python
import functools

import jax
import jax.numpy as jnp
from jax import lax
from jax.experimental import pallas as pl
from jax.experimental.pallas import tpu as pltpu
from jax.sharding import PartitionSpec as P

root_three = 1.7320508075688772
half_log_tau = 0.9189385332046727
LANES = 128
SUBLANES = 8
AXES = ("pts", "grp")


def lane_gather(row, index):
    return jnp.take_along_axis(row, index, axis=1, mode="promise_in_bounds")


def tile_of(ref, row):
    return jnp.broadcast_to(ref[pl.ds(row, 1), :], (SUBLANES, LANES))


def gather_members(all_ref, slot_ref, table_ref, far_index, far_rows, singles, doubles, scales):
    owners, capacity = table_ref.shape
    count, local = slot_ref.shape
    groups = local // LANES
    channels = 4
    rows_each = channels * groups
    near_slots = 3 * local
    tile_id, slab_id = lax.axis_index("pts"), lax.axis_index("grp")
    n_tiles, n_slabs = lax.axis_size("pts"), lax.axis_size("grp")
    device = tile_id * n_slabs + slab_id

    far_index[...] = jnp.zeros(far_index.shape, jnp.int32)
    far_index[:, :capacity] = table_ref[...]
    for base in range(0, owners, SUBLANES):
        index = far_index[base : base + SUBLANES, :]
        lane, chunk = index & (LANES - 1), index >> 7
        for c in range(channels):
            value = None
            for g in range(groups):
                source = all_ref[pl.ds(base * rows_each + c * groups + g, SUBLANES, stride=rows_each), :]
                picked = lane_gather(source, lane)
                value = picked if value is None else jnp.where(chunk == g, picked, value)
            far_rows[c, base : base + SUBLANES, :] = value

    neighbours = [
        jnp.maximum(tile_id - 1, 0) * n_slabs + slab_id,
        device,
        jnp.minimum(tile_id + 1, n_tiles - 1) * n_slabs + slab_id,
    ]
    starts = list(range(0, count - SUBLANES + 1, SUBLANES))
    if starts[-1] + SUBLANES < count:
        starts.append(count - SUBLANES)
    for first in starts:
        slots = [slot_ref[first : first + SUBLANES, g * LANES : (g + 1) * LANES] for g in range(groups)]
        lanes = [s & (LANES - 1) for s in slots]
        chunks = [s >> 7 for s in slots]
        found = [[None] * channels for _ in range(groups)]
        for t in range(3):
            for q in range(groups):
                tables = [tile_of(all_ref, neighbours[t] * rows_each + c * groups + q) for c in range(channels)]
                for g in range(groups):
                    here = chunks[g] == t * groups + q
                    for c in range(channels):
                        picked = lane_gather(tables[c], lanes[g])
                        old = found[g][c]
                        found[g][c] = picked if old is None else jnp.where(here, picked, old)

        far = slots[0] - near_slots

        def one_owner(o, carry):
            place = far - o * capacity
            here = (place >= 0) & (place < capacity)
            lane = place & (LANES - 1)
            return tuple(
                jnp.where(here, lane_gather(tile_of(far_rows.at[c], o), lane), carry[c]) for c in range(channels)
            )

        found[0] = list(lax.fori_loop(0, owners, one_owner, tuple(found[0]), unroll=8))
        for g in range(groups):
            for c in range(channels):
                value = found[g][c]
                if c < 3:
                    value = value * scales[c]
                    singles[c, pl.ds(first * groups + g, SUBLANES, stride=groups), :] = value
                for half in range(2):
                    start = first * SUBLANES + half * groups + g
                    doubles[c, pl.ds(start, SUBLANES, stride=SUBLANES), :] = value
    for c in range(channels):
        own = all_ref[pl.ds(device * rows_each + c * groups, groups), :]
        if c < 3:
            own = own * scales[c][:groups]
            singles[c, count * groups : (count + 1) * groups, :] = own
            singles[c, (count + 1) * groups : (count + 2) * groups, :] = own
        for half in range(2):
            start = count * SUBLANES + half * groups
            doubles[c, start : start + groups, :] = own


def kernel(all_ref, slot_ref, table_ref, lengths, nugget, white_ref, part_ref, far_index, far_rows, singles, doubles, final, scaled):
    count, local = slot_ref.shape
    groups = local // LANES
    order = count + 1
    pairs = (order + 1) // 2
    full = (SUBLANES, LANES)
    scales = [root_three / jnp.full(full, lengths[c], jnp.float32) for c in range(3)]
    gather_members(all_ref, slot_ref, table_ref, far_index, far_rows, singles, doubles, scales)

    low = lax.broadcasted_iota(jnp.int32, full, 0) < groups
    diagonal = jnp.full(full, 1.0 + nugget[0], jnp.float32)

    def single(c, j):
        return singles[c, j * SUBLANES : (j + 1) * SUBLANES, :]

    def double(c, a):
        return doubles[c, a * SUBLANES : (a + 1) * SUBLANES, :]

    def entry(a, j):
        if j == a // 2 and a % 2 == 1:
            return diagonal
        if j == a // 2 and a == order - 1:
            return jnp.where(low, diagonal, double(3, a))
        square = None
        for c in range(3):
            gap = double(c, a) - single(c, j)
            square = gap * gap if square is None else square + gap * gap
        distance = square * lax.rsqrt(jnp.maximum(square, 1e-35))
        value = (1.0 + distance) * jnp.exp(-distance)
        if j == a // 2:
            value = jnp.where(low, diagonal, value)
        if j == pairs - 1:
            value = jnp.where(low, value, double(3, a))
        return value

    def both(value, half):
        other = pltpu.roll(value, groups, 0)
        return jnp.where(low, value, other) if half == 0 else jnp.where(low, other, value)

    def final_at(k, j):
        return pl.ds((k * pairs + j) * SUBLANES, SUBLANES)

    def scaled_at(k, a):
        return pl.ds((k * order + a) * SUBLANES, SUBLANES)

    block, span = 4, 8
    for top in range(0, order, block):
        rows = range(top, min(top + block, order))
        values = {}
        for begin in range(top // 2, pairs, span):
            columns = range(begin, min(begin + span, pairs))
            held = {(a, j): entry(a, j) for a in rows for j in columns if j >= a // 2}
            for k in range(top):
                factors = {a: scaled[scaled_at(k, a), :] for a in rows}
                for j in columns:
                    row = final[final_at(k, j), :]
                    for a in rows:
                        if j >= a // 2:
                            held[a, j] = held[a, j] - factors[a] * row
            for a in rows:
                for k in range(top, a):
                    factor = values[k, a] if (k, a) in values else None
                    if factor is None:
                        factor = both(held[k, a // 2] * values[k], a % 2)
                        values[k, a] = factor
                    for j in columns:
                        if j >= a // 2:
                            held[a, j] = held[a, j] - factor * held[k, j]
                if a not in values:
                    values[a] = 1.0 / both(held[a, a // 2], a % 2)
            for a in rows:
                for j in columns:
                    if j < a // 2:
                        continue
                    value = held[a, j]
                    if a == order - 1:
                        pivot, solved = value, pltpu.roll(value, groups, 0)
                        white = solved * lax.rsqrt(pivot)
                        white_ref[...] = white[:groups]
                        term = jnp.log(pivot) + white * white
                        term = jnp.where(low, term, 0.0)
                        total = jnp.sum(term, axis=0, keepdims=True)
                        part_ref[...] = jnp.broadcast_to(total, part_ref.shape)
                        continue
                    final[final_at(a, j), :] = value
                    times = value * values[a]
                    swapped = pltpu.roll(times, groups, 0)
                    for half in range(2):
                        column = 2 * j + half
                        if top + block <= column < order:
                            pick = jnp.where(low, times, swapped) if half == 0 else jnp.where(low, swapped, times)
                            scaled[scaled_at(a, column), :] = pick


def body(coords, observations, length_scales, nugget, fetch_table, slot_of):
    local = coords.shape[1]
    owners, capacity = fetch_table.shape[1:]
    count = slot_of.shape[0]
    groups = local // LANES
    order = count + 1
    pairs = (order + 1) // 2
    assert 2 * groups == SUBLANES and order % 2 == 1 and capacity <= LANES
    devices = lax.axis_size("pts") * lax.axis_size("grp")
    payload = jnp.concatenate([coords, observations[None, :]], axis=0).reshape(4 * groups, LANES)
    everything = jnp.broadcast_to(payload[None], (devices, 4 * groups, LANES))
    everything = lax.all_to_all(everything, AXES, split_axis=0, concat_axis=0, tiled=True)
    vmem = pl.BlockSpec(memory_space=pltpu.VMEM)
    smem = pl.BlockSpec(memory_space=pltpu.SMEM)
    white, part = pl.pallas_call(
        kernel,
        out_shape=(
            jax.ShapeDtypeStruct((groups, LANES), jnp.float32),
            jax.ShapeDtypeStruct((devices, LANES), jnp.float32),
        ),
        in_specs=[vmem, vmem, vmem, smem, smem],
        out_specs=(vmem, vmem),
        scratch_shapes=[
            pltpu.VMEM((owners, LANES), jnp.int32),
            pltpu.VMEM((4, owners, LANES), jnp.float32),
            pltpu.VMEM((3, pairs * SUBLANES, LANES), jnp.float32),
            pltpu.VMEM((4, order * SUBLANES, LANES), jnp.float32),
            pltpu.VMEM((order * pairs * SUBLANES, LANES), jnp.float32),
            pltpu.VMEM((order * order * SUBLANES, LANES), jnp.float32),
        ],
    )(everything.reshape(devices * 4 * groups, LANES), slot_of, fetch_table[0], length_scales, nugget)
    parts = lax.all_to_all(part, AXES, split_axis=0, concat_axis=0, tiled=True)
    neg_loglik = jnp.sum(parts) / (2.0 * local * devices) + half_log_tau
    return (white.reshape(local), neg_loglik)


def solution(mesh):
    in_specs = (P(None, AXES), P(AXES), P(), P(), P(AXES, None, None), P(None, AXES))
    out_specs = (P(AXES), P())
    return jax.shard_map(body, mesh=mesh, in_specs=in_specs, out_specs=out_specs, check_vma=False)
```

time: 147 us -> 40.1 us (0.27); the launches traced: 144 us -> 39.7 us
  matrix products: 30.6 us -> 0 us
  local copies, waits for them, and re-layouts: 30.2 us -> 1.41 us
  blocking collectives: 38.4 us -> 9.63 us
  other arithmetic: 10.8 us -> 1.36 us
  starting transfers between devices: 15.6 us -> 7.33 us
  Pallas kernels: 0 us -> 6.99 us
  waiting for transfers between devices: 12.8 us -> 9.93 us
  between operations: 4.68 us -> 3.07 us
    psum x1 -> x0, blocking collectives: 38.4 us -> none  [body(): total = lax.psum(partial_value, ('pts', 'grp'))]
    dot_general x30 -> x0, matrix products: 30.6 us -> none  [one_neighbour(): product = jnp.dot(pieces, picker, preferred_element_type=jnp.float32)]
    dynamic_slice x30 -> x0, local copies, waits for them, and re-layouts: 21.8 us -> none  [select_slots(): picked = lax.map(one_neighbour, slot_of)]
    all_to_all x0 -> x1, blocking collectives: none -> 9.63 us  [body(): parts = lax.all_to_all(part, AXES, split_axis=0, concat_axis=0, tiled=True)]
    pallas_call x0 -> x1, Pallas kernels: none -> 6.99 us  [body(): pl.pallas_call(kernel, out_shape=(jax.ShapeDtypeStruct((groups, LANES), j...]
    ppermute x2 -> x0, starting transfers between devices: 6.81 us -> none  [the longest x1 5.53 us: extended(): lax.ppermute(tail, axis, [(i, (i + 1) % count) for i in range(ends)])]
    sub x59 -> x0, other arithmetic: 4.74 us -> none  [the longest x29 4.26 us: eliminate(): matrix = matrix[1:, 1:] - column[:, None, :] * column[None, :, :]]
    gather x3 -> x0, local copies, waits for them, and re-layouts: 3.02 us -> none  [body(): served = jnp.take(payload, wanted, axis=1)]
  transfers between devices with their start and end apart: 4 -> 1, of which waited for: 2 -> 1; matrix products, arithmetic and copies ran while one was open for 4% -> 0% of each run, Pallas kernels for 0% -> 0%
where the time goes in v1:
time: 40.1 us; the launch traced here: 39.7 us
  waiting for transfers between devices  9.93 us (25%)
  blocking collectives  9.63 us (24%)
  starting transfers between devices  7.33 us (18%)
  Pallas kernels  6.99 us (17%)
  between operations  3.07 us (8%)
  local copies, waits for them, and re-layouts  1.41 us (4%)
  other arithmetic  1.36 us (3%)
    all_to_all x1, waiting for transfers between devices, body(): lax.all_to_all(everything, AXES, split_axis=0, concat_axis=0, tiled=True)  9.93 us
    all_to_all x1, blocking collectives, body(): parts = lax.all_to_all(part, AXES, split_axis=0, concat_axis=0, tiled=True)  9.63 us
    all_to_all x1, starting transfers between devices, body(): lax.all_to_all(everything, AXES, split_axis=0, concat_axis=0, tiled=True)  7.33 us
    pallas_call x1, Pallas kernels, body(): pl.pallas_call(kernel, out_shape=(jax.ShapeDtypeStruct((groups, LANES), j...  6.99 us
  transfers between devices with their start and end apart: 1, of which 1 were waited for; matrix products, arithmetic and copies ran while one was open for 0% of the time, Pallas kernels for 0%

profile of v1, /device:TPU:0, one launch (start us, length us, event | category | flops | bytes accessed | tf_op | source)
XLA Modules:
  0.0 39.7 jit_solution(12680772707087989491)
XLA Ops:
  0.6 0.7 %pad_maximum_fusion = f32[4,512]{1,0:T(4,128)S(1)} fusion(f32[1,512]{1,0:T(1,128)} %bitcast.10, f32[3,512]{1,0:T(4,128)} %param.6), kind=kLoop, calls=%fused_computation | loop fusion | flops 2048 | bytes 16384 | tf_op jit(solution)/shard_map/concatenate | solution.py:206
  1.4 0.7 %broadcast_in_dim.12 = f32[32,16,128]{2,1,0:T(8,128)} broadcast(f32[16,128]{1,0:T(8,128)S(1)} %broadcast_in_dim.11), dimensions={1,2} | broadcast | bytes 270336 | tf_op jit(solution)/shard_map/broadcast_in_dim | solution.py:207
  2.1 7.3 %all-to-all-start = ((f32[32,16,128]{2,1,0:T(8,128)}), f32[32,16,128]{2,1,0:T(8,128)S(1)}, u32[]{:S(2)}, u32[]{:S(2)}) async-start(f32[32,16,128]{2,1,0:T(8,128)} %broadcast_in_dim.12), calls=%async_computation | async-start | bytes 524288 | tf_op jit(solution)/shard_map/all_to_all | solution.py:208
  10.1 9.9 %all-to-all-done = f32[32,16,128]{2,1,0:T(8,128)S(1)} async-done(((f32[32,16,128]{2,1,0:T(8,128)}), f32[32,16,128]{2,1,0:T(8,128)S(1)}, u32[]{:S(2)}, u32[]{:S(2)}) %all-to-all-start) | async-done | bytes 262176 | tf_op jit(solution)/shard_map/all_to_all | solution.py:208
  20.0 0.0 copy-start
  20.0 0.7 %copy-done = f32[32,16,128]{2,1,0:T(8,128)} copy-done((f32[32,16,128]{2,1,0:T(8,128)}, f32[32,16,128]{2,1,0:T(8,128)S(1)}, u32[]{:S(2)}) %copy-start) | copy-done | bytes 262168
  20.7 7.0 %shard_map.77 = (f32[4,128]{1,0:T(4,128)}, f32[32,128]{1,0:T(8,128)}) custom-call(f32[512,128]{1,0:T(8,128)} %bitcast.7, s32[30,512]{1,0:T(8,128)} %slot_ref.1, s32[32,41]{1,0:T(8,128)} %bitcast.9, f32[3]{0:T(128)} %lengths.1, f32[1]{0:T(128)S(6)} %copy.9.nugget), custom_call_target="tpu_custom_call" | custom-call | tf_op jit(solution)/shard_map/pallas_call | solution.py:211
  27.7 9.6 %all_to_all.14 = f32[32,1,128]{2,1,0:T(1,128)S(1)} all-to-all(f32[32,1,128]{2,1,0:T(1,128)} %bitcast.8), channel_id=1, replica_groups=mesh['pts'=8,'grp'=4] {'pts','grp'}, dimensions={0} | all-to-all | bytes 32768 | tf_op jit(solution)/shard_map/all_to_all | solution.py:228
  37.3 0.6 %reduce_sum.9 = f32[]{:T(128)} reduce(f32[32,1,128]{2,1,0:T(1,128)S(1)} %all_to_all.14, f32[]{:T(128)} %constant.1.clone.1), dimensions={0,1,2}, to_apply=%region_0.0 | reduce | flops 4095 | bytes 16392 | tf_op jit(solution)/shard_map/reduce_sum | solution.py:229
  (1 shorter events, 0.0 us)
Async XLA Ops:
  2.1 17.9 %all-to-all-start = ((f32[32,16,128]{2,1,0:T(8,128)}), f32[32,16,128]{2,1,0:T(8,128)S(1)}, u32[]{:S(2)}, u32[]{:S(2)}) async-start(f32[32,16,128]{2,1,0:T(8,128)} %broadcast_in_dim.12), calls=%async_computation | async-start | bytes 524288 | tf_op jit(solution)/shard_map/all_to_all | solution.py:208
  20.0 0.7 %copy-start = (f32[32,16,128]{2,1,0:T(8,128)}, f32[32,16,128]{2,1,0:T(8,128)S(1)}, u32[]{:S(2)}) copy-start(f32[32,16,128]{2,1,0:T(8,128)S(1)} %all-to-all-done) | copy-start | bytes 786436

commit v2 on v1

v2 whole, which is shorter than its diff:
```python
import jax
import jax.numpy as jnp
from jax import lax
from jax.experimental import pallas as pl
from jax.experimental.pallas import tpu as pltpu
from jax.sharding import PartitionSpec as P

root_three = 1.7320508075688772
minus_log2_e = -1.4426950408889634
half_log_tau = 0.9189385332046727
LANES = 128
SUBLANES = 8
CHANNELS = 4
EARLY = 32
AXES = ("pts", "grp")


def lane_gather(row, index):
    return jnp.take_along_axis(row, index, axis=1, mode="promise_in_bounds")


def tile_of(ref, row):
    return jnp.broadcast_to(ref[pl.ds(row, 1), :], (SUBLANES, LANES))


def kernel(all_ref, slot_ref, table_ref, scalars, white_ref, part_ref,
           slots, far_index, far_rows, singles, doubles, final, scaled, inverses):
    owners, capacity = table_ref.shape
    count, local = slot_ref.shape
    groups = local // LANES
    rows_each = CHANNELS * groups
    near_slots = 3 * local
    order = count + 1
    pairs = (order + 1) // 2
    panels = pairs * 2 // SUBLANES
    full = (SUBLANES, LANES)
    tile_id, slab_id = lax.axis_index("pts"), lax.axis_index("grp")
    n_tiles, n_slabs = lax.axis_size("pts"), lax.axis_size("grp")
    device = tile_id * n_slabs + slab_id
    scales = [root_three / jnp.full(full, scalars[c], jnp.float32) for c in range(3)]
    low = lax.broadcasted_iota(jnp.int32, full, 0) < groups
    lane_id = lax.broadcasted_iota(jnp.int32, full, 1)
    diagonal = jnp.full(full, 1.0 + scalars[3], jnp.float32)

    far_index[...] = jnp.zeros(far_index.shape, jnp.int32)
    far_index[:, :capacity] = table_ref[...]
    for base in range(0, owners, SUBLANES):
        index = far_index[base : base + SUBLANES, :]
        lane, chunk = index & (LANES - 1), index >> 7
        for c in range(CHANNELS):
            value = None
            for g in range(groups):
                source = all_ref[pl.ds(base * rows_each + g * CHANNELS + c, SUBLANES, stride=rows_each), :]
                picked = lane_gather(source, lane)
                value = picked if value is None else jnp.where(chunk == g, picked, value)
            far_rows[c, base : base + SUBLANES, :] = value

    slots[count:, :] = jnp.zeros((slots.shape[0] - count, local), jnp.int32)
    slots[:count, :] = slot_ref[...]

    packed = slots[:SUBLANES, :LANES]
    for p in range(1, panels):
        moved = pltpu.roll(slots[p * SUBLANES : (p + 1) * SUBLANES, :LANES], p * EARLY, 1)
        packed = jnp.where(lane_id < p * EARLY, packed, moved)
    place = packed - near_slots
    far = [jnp.zeros(full, jnp.float32)] * CHANNELS
    for o in range(owners):
        here = (place >= 0) & (place < capacity)
        lane = place & (LANES - 1)
        for c in range(CHANNELS):
            far[c] = jnp.where(here, lane_gather(tile_of(far_rows.at[c], o), lane), far[c])
        place = place - capacity

    neighbours = [
        jnp.maximum(tile_id - 1, 0) * n_slabs + slab_id,
        device,
        jnp.minimum(tile_id + 1, n_tiles - 1) * n_slabs + slab_id,
    ]

    def gather(p):
        first = p * SUBLANES
        mine = [slots[first : first + SUBLANES, g * LANES : (g + 1) * LANES] for g in range(groups)]
        lanes = [s & (LANES - 1) for s in mine]
        chunks = [s >> 7 for s in mine]
        found = [[None] * CHANNELS for _ in range(groups)]
        for t in range(3):
            for q in range(groups):
                tables = [tile_of(all_ref, neighbours[t] * rows_each + q * CHANNELS + c) for c in range(CHANNELS)]
                for g in range(groups):
                    here = chunks[g] == t * groups + q
                    for c in range(CHANNELS):
                        picked = lane_gather(tables[c], lanes[g])
                        old = found[g][c]
                        found[g][c] = picked if old is None else jnp.where(here, picked, old)
        distant = mine[0] >= near_slots
        for c in range(CHANNELS):
            moved = pltpu.roll(far[c], LANES - p * EARLY, 1) if p else far[c]
            found[0][c] = jnp.where(distant, moved, found[0][c])
        for g in range(groups):
            for c in range(CHANNELS):
                value = found[g][c]
                if c < 3:
                    value = value * scales[c]
                    singles[c, pl.ds(first * groups + g, SUBLANES, stride=groups), :] = value
                for half in range(2):
                    start = first * SUBLANES + half * groups + g
                    doubles[c, pl.ds(start, SUBLANES, stride=SUBLANES), :] = value
        if p == panels - 1:
            for c in range(CHANNELS):
                own = all_ref[pl.ds(device * rows_each + c, groups, stride=CHANNELS), :]
                if c < 3:
                    own = own * scales[c][:groups]
                    singles[c, count * groups : (count + 1) * groups, :] = own
                for half in range(2):
                    start = count * SUBLANES + half * groups
                    doubles[c, start : start + groups, :] = own

    def single(c, j):
        return singles[c, j * SUBLANES : (j + 1) * SUBLANES, :]

    def double(c, a):
        return doubles[c, a * SUBLANES : (a + 1) * SUBLANES, :]

    def entry(a, j):
        if j == a // 2 and a % 2 == 1:
            return diagonal
        if j == a // 2 and a == order - 1:
            return jnp.where(low, diagonal, double(3, a))
        square = None
        for c in range(3):
            gap = double(c, a) - single(c, j)
            square = gap * gap if square is None else square + gap * gap
        distance = square * lax.rsqrt(jnp.maximum(square, 1e-35))
        value = (1.0 + distance) * jnp.exp2(distance * minus_log2_e)
        if j == a // 2:
            value = jnp.where(low, diagonal, value)
        if j == pairs - 1:
            value = jnp.where(low, value, double(3, a))
        return value

    def halves(value):
        other = pltpu.roll(value, groups, 0)
        return jnp.where(low, value, other), jnp.where(low, other, value)

    def final_at(k, j):
        return pl.ds((k * pairs + j) * SUBLANES, SUBLANES)

    def scaled_at(k, a):
        return pl.ds((k * order + a) * SUBLANES, SUBLANES)

    block = 4

    def eliminate(p):
        columns = range(p * SUBLANES // 2, (p + 1) * SUBLANES // 2)
        start = p * SUBLANES
        for top in range(0, min(start + SUBLANES, order), block):
            rows = range(top, min(top + block, order))
            held = {(a, j): entry(a, j) for a in rows for j in columns if j >= a // 2}
            for k in range(top):
                factors = {a: scaled[scaled_at(k, a), :] for a in rows}
                for j in columns:
                    row = final[final_at(k, j), :]
                    for a in rows:
                        if j >= a // 2:
                            held[a, j] = held[a, j] - factors[a] * row
            made = {}
            for a in rows:
                for k in range(top, a):
                    factor = made[k, a] if (k, a) in made else scaled[scaled_at(k, a), :]
                    for j in columns:
                        if j >= a // 2:
                            held[a, j] = held[a, j] - factor * held[k, j]
                if a == order - 1:
                    pivot = held[a, pairs - 1]
                    white = pltpu.roll(pivot, groups, 0) * lax.rsqrt(pivot)
                    white_ref[...] = white[:groups]
                    term = jnp.where(low, jnp.log(pivot) + white * white, 0.0)
                    total = jnp.sum(term, axis=0, keepdims=True)
                    part_ref[...] = jnp.broadcast_to(total, part_ref.shape)
                    break
                if a >= start:
                    inverse = 1.0 / halves(held[a, a // 2])[a % 2]
                    inverses[a * SUBLANES : (a + 1) * SUBLANES, :] = inverse
                else:
                    inverse = inverses[a * SUBLANES : (a + 1) * SUBLANES, :]
                for j in columns:
                    if j < a // 2:
                        continue
                    final[final_at(a, j), :] = held[a, j]
                    if 2 * j + 1 <= a:
                        continue
                    pair = halves(held[a, j] * inverse)
                    for half in range(2):
                        m = 2 * j + half
                        if a < m < order:
                            made[a, m] = pair[half]
                            scaled[scaled_at(a, m), :] = pair[half]

    gather(0)
    for p in range(panels):
        if p + 1 < panels:
            gather(p + 1)
        eliminate(p)


def body(coords, observations, length_scales, nugget, fetch_table, slot_of):
    local = coords.shape[1]
    owners, capacity = fetch_table.shape[1:]
    count = slot_of.shape[0]
    groups = local // LANES
    order = count + 1
    pairs = (order + 1) // 2
    panels = pairs * 2 // SUBLANES
    assert 2 * groups == SUBLANES and (order + 1) % SUBLANES == 0
    assert capacity <= LANES and panels * EARLY <= LANES
    devices = lax.axis_size("pts") * lax.axis_size("grp")
    payload = jnp.concatenate([coords, observations[None, :]], axis=0)
    everything = jnp.broadcast_to(payload[None], (devices, CHANNELS, local))
    everything = lax.all_to_all(everything, AXES, split_axis=0, concat_axis=0, tiled=True)
    everything = everything.reshape(devices, CHANNELS, groups, LANES).transpose(0, 2, 1, 3)
    scalars = jnp.concatenate([length_scales, nugget])
    vmem = pl.BlockSpec(memory_space=pltpu.VMEM)
    smem = pl.BlockSpec(memory_space=pltpu.SMEM)
    white, part = pl.pallas_call(
        kernel,
        out_shape=(
            jax.ShapeDtypeStruct((groups, LANES), jnp.float32),
            jax.ShapeDtypeStruct((devices, LANES), jnp.float32),
        ),
        in_specs=[vmem, vmem, vmem, smem],
        out_specs=(vmem, vmem),
        scratch_shapes=[
            pltpu.VMEM((panels * SUBLANES, local), jnp.int32),
            pltpu.VMEM((owners, LANES), jnp.int32),
            pltpu.VMEM((CHANNELS, owners, LANES), jnp.float32),
            pltpu.VMEM((3, pairs * SUBLANES, LANES), jnp.float32),
            pltpu.VMEM((CHANNELS, 2 * pairs * SUBLANES, LANES), jnp.float32),
            pltpu.VMEM((order * pairs * SUBLANES, LANES), jnp.float32),
            pltpu.VMEM((order * order * SUBLANES, LANES), jnp.float32),
            pltpu.VMEM((order * SUBLANES, LANES), jnp.float32),
        ],
        compiler_params=pltpu.CompilerParams(vmem_limit_bytes=16 << 20),
    )(everything.reshape(devices * CHANNELS * groups, LANES), slot_of, fetch_table[0], scalars)
    parts = lax.all_to_all(part, AXES, split_axis=0, concat_axis=0, tiled=True)
    neg_loglik = jnp.sum(parts) / (2.0 * local * devices) + half_log_tau
    return (white.reshape(local), neg_loglik)


def solution(mesh):
    in_specs = (P(None, AXES), P(AXES), P(), P(), P(AXES, None, None), P(None, AXES))
    out_specs = (P(AXES), P())
    return jax.shard_map(body, mesh=mesh, in_specs=in_specs, out_specs=out_specs, check_vma=False)
```

time: 40.1 us -> 36.2 us (0.903)
  Pallas kernels: 6.99 us -> 4.12 us
  local copies, waits for them, and re-layouts: 1.41 us -> 0.74 us
    pallas_call x1, Pallas kernels: 6.99 us -> 4.12 us  [body(): pl.pallas_call(kernel, out_shape=(jax.ShapeDtypeStruct((groups, LANES), j...]
    unnamed x2 -> x6, local copies, waits for them, and re-layouts: 0.69 us -> 0.01 us
where the time goes in v2:
time: 36.2 us; the launch traced here: 35.9 us
  waiting for transfers between devices  9.82 us (27%)
  blocking collectives  9.37 us (26%)
  starting transfers between devices  7.33 us (20%)
  Pallas kernels  4.12 us (11%)
  between operations  3.09 us (9%)
  other arithmetic  1.43 us (4%)
  local copies, waits for them, and re-layouts  0.74 us (2%)
    all_to_all x1, waiting for transfers between devices, body(): lax.all_to_all(everything, AXES, split_axis=0, concat_axis=0, tiled=True)  9.82 us
    all_to_all x1, blocking collectives, body(): parts = lax.all_to_all(part, AXES, split_axis=0, concat_axis=0, tiled=True)  9.37 us
    all_to_all x1, starting transfers between devices, body(): lax.all_to_all(everything, AXES, split_axis=0, concat_axis=0, tiled=True)  7.33 us
    pallas_call x1, Pallas kernels, body(): pl.pallas_call(kernel, out_shape=(jax.ShapeDtypeStruct((groups, LANES), j...  4.12 us
    broadcast_in_dim x1, local copies, waits for them, and re-layouts, body(): everything = jnp.broadcast_to(payload[None], (devices, CHANNELS, local))  0.73 us
  transfers between devices with their start and end apart: 1, of which 1 were waited for; matrix products, arithmetic and copies ran while one was open for 0% of the time, Pallas kernels for 0%

profile of v2, /device:TPU:0, one launch (start us, length us, event | category | flops | bytes accessed | tf_op | source)
XLA Modules:
  0.0 35.9 jit_solution(17838856794435322880)
XLA Ops:
  0.6 0.7 %pad_maximum_fusion = f32[4,512]{1,0:T(4,128)S(1)} fusion(f32[1,512]{1,0:T(1,128)} %bitcast.14, f32[3,512]{1,0:T(4,128)} %param.6), kind=kLoop, calls=%fused_computation | loop fusion | flops 2048 | bytes 16384 | tf_op jit(solution)/shard_map/concatenate | solution.py:217
  1.4 0.7 %broadcast_in_dim.10 = f32[32,4,512]{2,1,0:T(4,128)} broadcast(f32[4,512]{1,0:T(4,128)S(1)} %pad_maximum_fusion), dimensions={1,2} | broadcast | bytes 270336 | tf_op jit(solution)/shard_map/broadcast_in_dim | solution.py:218
  2.1 0.0 copy-start
  2.1 0.0 copy-start.1
  2.1 7.3 %all-to-all-start = ((f32[32,4,512]{2,1,0:T(4,128)}), f32[32,4,512]{2,1,0:T(4,128)S(1)}, u32[]{:S(2)}, u32[]{:S(2)}) async-start(f32[32,4,512]{2,1,0:T(4,128)} %broadcast_in_dim.10), calls=%async_computation | async-start | bytes 524288 | tf_op jit(solution)/shard_map/all_to_all | solution.py:219
  9.4 0.0 copy-start.2
  10.1 0.0 copy-done.2
  10.1 0.1 pad_maximum_fusion.1.scalars
  10.2 9.8 %all-to-all-done = f32[32,4,512]{2,1,0:T(4,128)S(1)} async-done(((f32[32,4,512]{2,1,0:T(4,128)}), f32[32,4,512]{2,1,0:T(4,128)S(1)}, u32[]{:S(2)}, u32[]{:S(2)}) %all-to-all-start) | async-done | bytes 262176 | tf_op jit(solution)/shard_map/all_to_all | solution.py:219
  20.0 0.0 copy-done
  20.0 0.0 copy-done.1
  20.0 4.1 %shard_map.77 = (f32[4,128]{1,0:T(4,128)}, f32[32,128]{1,0:T(8,128)S(1)}) custom-call(f32[512,128]{1,0:T(8,128)S(1)} %bitcast.11, s32[30,512]{1,0:T(8,128)S(1)} %copy-done, s32[32,41]{1,0:T(8,128)S(1)} %bitcast.13, f32[4]{0:T(128)S(1)} %pad_maximum_fusion.1.scalars), custom_call_target="tpu_custom_call" | custom-call | tf_op jit(solution)/shard_map/pallas_call | solution.py:224
  24.1 9.4 %all_to_all.14 = f32[32,1,128]{2,1,0:T(1,128)S(1)} all-to-all(f32[32,1,128]{2,1,0:T(1,128)S(1)} %bitcast.12), channel_id=1, replica_groups=mesh['pts'=8,'grp'=4] {'pts','grp'}, dimensions={0} | all-to-all | bytes 32768 | tf_op jit(solution)/shard_map/all_to_all | solution.py:244
  33.5 0.6 %reduce_sum.9 = f32[]{:T(128)} reduce(f32[32,1,128]{2,1,0:T(1,128)S(1)} %all_to_all.14, f32[]{:T(128)} %constant.1.clone.1), dimensions={0,1,2}, to_apply=%region_0.0 | reduce | flops 4095 | bytes 16392 | tf_op jit(solution)/shard_map/reduce_sum | solution.py:245
Async XLA Ops:
  2.1 17.9 %copy-start = (s32[30,512]{1,0:T(8,128)S(1)}, s32[30,512]{1,0:T(8,128)}, u32[]{:S(2)}) copy-start(s32[30,512]{1,0:T(8,128)} %slot_ref.1) | copy-start | bytes 184324
  2.1 17.9 %copy-start.1 = (s32[1,32,41]{2,1,0:T(8,128)S(1)}, s32[1,32,41]{2,1,0:T(8,128)}, u32[]{:S(2)}) copy-start(s32[1,32,41]{2,1,0:T(8,128)} %param.10) | copy-start | bytes 15748
  2.1 17.9 %all-to-all-start = ((f32[32,4,512]{2,1,0:T(4,128)}), f32[32,4,512]{2,1,0:T(4,128)S(1)}, u32[]{:S(2)}, u32[]{:S(2)}) async-start(f32[32,4,512]{2,1,0:T(4,128)} %broadcast_in_dim.10), calls=%async_computation | async-start | bytes 524288 | tf_op jit(solution)/shard_map/all_to_all | solution.py:219
  9.4 0.7 %copy-start.2 = (f32[3]{0:T(128)S(1)}, f32[3]{0:T(128)}, u32[]{:S(2)}) copy-start(f32[3]{0:T(128)} %param.8) | copy-start | bytes 40

commit v3 on v2

--- a/solution.py
+++ b/solution.py
@@ -37,10 +37,10 @@
     tile_id, slab_id = lax.axis_index("pts"), lax.axis_index("grp")
     n_tiles, n_slabs = lax.axis_size("pts"), lax.axis_size("grp")
     device = tile_id * n_slabs + slab_id
-    scales = [root_three / jnp.full(full, scalars[c], jnp.float32) for c in range(3)]
+    scales = [root_three / jnp.broadcast_to(scalars[:, c : c + 1], full) for c in range(3)]
     low = lax.broadcasted_iota(jnp.int32, full, 0) < groups
     lane_id = lax.broadcasted_iota(jnp.int32, full, 1)
-    diagonal = jnp.full(full, 1.0 + scalars[3], jnp.float32)
+    diagonal = 1.0 + jnp.broadcast_to(scalars[:, 3:4], full)
 
     far_index[...] = jnp.zeros(far_index.shape, jnp.int32)
     far_index[:, :capacity] = table_ref[...]
@@ -77,35 +77,31 @@
         jnp.minimum(tile_id + 1, n_tiles - 1) * n_slabs + slab_id,
     ]
 
-    def gather(p):
+    def gather(p, g):
         first = p * SUBLANES
-        mine = [slots[first : first + SUBLANES, g * LANES : (g + 1) * LANES] for g in range(groups)]
-        lanes = [s & (LANES - 1) for s in mine]
-        chunks = [s >> 7 for s in mine]
-        found = [[None] * CHANNELS for _ in range(groups)]
+        mine = slots[first : first + SUBLANES, g * LANES : (g + 1) * LANES]
+        lane, chunk = mine & (LANES - 1), mine >> 7
+        found = [None] * CHANNELS
         for t in range(3):
             for q in range(groups):
-                tables = [tile_of(all_ref, neighbours[t] * rows_each + q * CHANNELS + c) for c in range(CHANNELS)]
-                for g in range(groups):
-                    here = chunks[g] == t * groups + q
-                    for c in range(CHANNELS):
-                        picked = lane_gather(tables[c], lanes[g])
-                        old = found[g][c]
-                        found[g][c] = picked if old is None else jnp.where(here, picked, old)
-        distant = mine[0] >= near_slots
+                here = chunk == t * groups + q
+                for c in range(CHANNELS):
+                    picked = lane_gather(tile_of(all_ref, neighbours[t] * rows_each + q * CHANNELS + c), lane)
+                    found[c] = picked if found[c] is None else jnp.where(here, picked, found[c])
+        if g == 0:
+            distant = mine >= near_slots
+            for c in range(CHANNELS):
+                moved = pltpu.roll(far[c], LANES - p * EARLY, 1) if p else far[c]
+                found[c] = jnp.where(distant, moved, found[c])
         for c in range(CHANNELS):
-            moved = pltpu.roll(far[c], LANES - p * EARLY, 1) if p else far[c]
-            found[0][c] = jnp.where(distant, moved, found[0][c])
-        for g in range(groups):
-            for c in range(CHANNELS):
-                value = found[g][c]
-                if c < 3:
-                    value = value * scales[c]
-                    singles[c, pl.ds(first * groups + g, SUBLANES, stride=groups), :] = value
-                for half in range(2):
-                    start = first * SUBLANES + half * groups + g
-                    doubles[c, pl.ds(start, SUBLANES, stride=SUBLANES), :] = value
-        if p == panels - 1:
+            value = found[c]
+            if c < 3:
+                value = value * scales[c]
+                singles[c, pl.ds(first * groups + g, SUBLANES, stride=groups), :] = value
+            for half in range(2):
+                start = first * SUBLANES + half * groups + g
+                doubles[c, pl.ds(start, SUBLANES, stride=SUBLANES), :] = value
+        if p == panels - 1 and g == groups - 1:
             for c in range(CHANNELS):
                 own = all_ref[pl.ds(device * rows_each + c, groups, stride=CHANNELS), :]
                 if c < 3:
@@ -150,10 +146,13 @@
 
     block = 4
 
-    def eliminate(p):
+    def eliminate(p, waiting):
         columns = range(p * SUBLANES // 2, (p + 1) * SUBLANES // 2)
         start = p * SUBLANES
-        for top in range(0, min(start + SUBLANES, order), block):
+        tops = range(0, min(start + SUBLANES, order), block)
+        for step, top in enumerate(tops):
+            for part in waiting[step * len(waiting) // len(tops) : (step + 1) * len(waiting) // len(tops)]:
+                gather(*part)
             rows = range(top, min(top + block, order))
             held = {(a, j): entry(a, j) for a in rows for j in columns if j >= a // 2}
             for k in range(top):
@@ -196,11 +195,10 @@
                             made[a, m] = pair[half]
                             scaled[scaled_at(a, m), :] = pair[half]
 
-    gather(0)
+    for g in range(groups):
+        gather(0, g)
     for p in range(panels):
-        if p + 1 < panels:
-            gather(p + 1)
-        eliminate(p)
+        eliminate(p, [(p + 1, g) for g in range(groups)] if p + 1 < panels else [])
 
 
 def body(coords, observations, length_scales, nugget, fetch_table, slot_of):
@@ -218,16 +216,15 @@
     everything = jnp.broadcast_to(payload[None], (devices, CHANNELS, local))
     everything = lax.all_to_all(everything, AXES, split_axis=0, concat_axis=0, tiled=True)
     everything = everything.reshape(devices, CHANNELS, groups, LANES).transpose(0, 2, 1, 3)
-    scalars = jnp.concatenate([length_scales, nugget])
+    scalars = jnp.concatenate([length_scales, nugget])[None]
     vmem = pl.BlockSpec(memory_space=pltpu.VMEM)
-    smem = pl.BlockSpec(memory_space=pltpu.SMEM)
     white, part = pl.pallas_call(
         kernel,
         out_shape=(
             jax.ShapeDtypeStruct((groups, LANES), jnp.float32),
             jax.ShapeDtypeStruct((devices, LANES), jnp.float32),
         ),
-        in_specs=[vmem, vmem, vmem, smem],
+        in_specs=[vmem, vmem, vmem, vmem],
         out_specs=(vmem, vmem),
         scratch_shapes=[
             pltpu.VMEM((panels * SUBLANES, local), jnp.int32),

time: 36.2 us -> 35.4 us (0.978)
  Pallas kernels: 4.12 us -> 3.23 us
    pallas_call x1, Pallas kernels: 4.12 us -> 3.23 us  [body(): pl.pallas_call(kernel, out_shape=(jax.ShapeDtypeStruct((groups, LANES), j...]
where the time goes in v3:
time: 35.4 us; the launch traced here: 35 us
  waiting for transfers between devices  9.82 us (28%)
  blocking collectives  9.37 us (26%)
  starting transfers between devices  7.33 us (21%)
  Pallas kernels  3.23 us (9%)
  between operations  3.09 us (9%)
  other arithmetic  1.43 us (4%)
  local copies, waits for them, and re-layouts  0.74 us (2%)
    all_to_all x1, waiting for transfers between devices, body(): lax.all_to_all(everything, AXES, split_axis=0, concat_axis=0, tiled=True)  9.82 us
    all_to_all x1, blocking collectives, body(): parts = lax.all_to_all(part, AXES, split_axis=0, concat_axis=0, tiled=True)  9.37 us
    all_to_all x1, starting transfers between devices, body(): lax.all_to_all(everything, AXES, split_axis=0, concat_axis=0, tiled=True)  7.33 us
    pallas_call x1, Pallas kernels, body(): pl.pallas_call(kernel, out_shape=(jax.ShapeDtypeStruct((groups, LANES), j...  3.23 us
    broadcast_in_dim x1, local copies, waits for them, and re-layouts, body(): everything = jnp.broadcast_to(payload[None], (devices, CHANNELS, local))  0.73 us
    concatenate x1, other arithmetic, body(): payload = jnp.concatenate([coords, observations[None, :]], axis=0)  0.72 us
  transfers between devices with their start and end apart: 1, of which 1 were waited for; matrix products, arithmetic and copies ran while one was open for 0% of the time, Pallas kernels for 0%

profile of v3, /device:TPU:0, one launch (start us, length us, event | category | flops | bytes accessed | tf_op | source)
XLA Modules:
  0.0 35.0 jit_solution(10303098641626777653)
XLA Ops:
  0.6 0.7 %pad_maximum_fusion = f32[4,512]{1,0:T(4,128)S(1)} fusion(f32[1,512]{1,0:T(1,128)} %bitcast.16, f32[3,512]{1,0:T(4,128)} %param.6), kind=kLoop, calls=%fused_computation | loop fusion | flops 2048 | bytes 16384 | tf_op jit(solution)/shard_map/concatenate | solution.py:215
  1.4 0.7 %broadcast_in_dim.13 = f32[32,4,512]{2,1,0:T(4,128)} broadcast(f32[4,512]{1,0:T(4,128)S(1)} %pad_maximum_fusion), dimensions={1,2} | broadcast | bytes 270336 | tf_op jit(solution)/shard_map/broadcast_in_dim | solution.py:216
  2.1 0.0 copy-start
  2.1 0.0 copy-start.1
  2.1 7.3 %all-to-all-start = ((f32[32,4,512]{2,1,0:T(4,128)}), f32[32,4,512]{2,1,0:T(4,128)S(1)}, u32[]{:S(2)}, u32[]{:S(2)}) async-start(f32[32,4,512]{2,1,0:T(4,128)} %broadcast_in_dim.13), calls=%async_computation | async-start | bytes 524288 | tf_op jit(solution)/shard_map/all_to_all | solution.py:217
  9.4 0.0 copy-start.2
  10.1 0.0 copy-done.2
  10.1 0.1 maximum_bitcast_fusion.scalars
  10.2 9.8 %all-to-all-done = f32[32,4,512]{2,1,0:T(4,128)S(1)} async-done(((f32[32,4,512]{2,1,0:T(4,128)}), f32[32,4,512]{2,1,0:T(4,128)S(1)}, u32[]{:S(2)}, u32[]{:S(2)}) %all-to-all-start) | async-done | bytes 262176 | tf_op jit(solution)/shard_map/all_to_all | solution.py:217
  20.0 0.0 copy-done
  20.0 0.0 copy-done.1
  20.0 3.2 %shard_map.77 = (f32[4,128]{1,0:T(4,128)}, f32[32,128]{1,0:T(8,128)S(1)}) custom-call(f32[512,128]{1,0:T(8,128)S(1)} %bitcast.13, s32[30,512]{1,0:T(8,128)S(1)} %copy-done, s32[32,41]{1,0:T(8,128)S(1)} %bitcast.15, f32[1,4]{1,0:T(1,128)S(1)} %maximum_bitcast_fusion.scalars), custom_call_target="tpu_custom_call" | custom-call | tf_op jit(solution)/shard_map/pallas_call | solution.py:221
  23.2 9.4 %all_to_all.14 = f32[32,1,128]{2,1,0:T(1,128)S(1)} all-to-all(f32[32,1,128]{2,1,0:T(1,128)S(1)} %bitcast.14), channel_id=1, replica_groups=mesh['pts'=8,'grp'=4] {'pts','grp'}, dimensions={0} | all-to-all | bytes 32768 | tf_op jit(solution)/shard_map/all_to_all | solution.py:241
  32.6 0.6 %reduce_sum.9 = f32[]{:T(128)} reduce(f32[32,1,128]{2,1,0:T(1,128)S(1)} %all_to_all.14, f32[]{:T(128)} %constant.1.clone.1), dimensions={0,1,2}, to_apply=%region_0.0 | reduce | flops 4095 | bytes 16392 | tf_op jit(solution)/shard_map/reduce_sum | solution.py:242
Async XLA Ops:
  2.1 17.9 %copy-start = (s32[30,512]{1,0:T(8,128)S(1)}, s32[30,512]{1,0:T(8,128)}, u32[]{:S(2)}) copy-start(s32[30,512]{1,0:T(8,128)} %slot_ref.1) | copy-start | bytes 184324
  2.1 17.9 %copy-start.1 = (s32[1,32,41]{2,1,0:T(8,128)S(1)}, s32[1,32,41]{2,1,0:T(8,128)}, u32[]{:S(2)}) copy-start(s32[1,32,41]{2,1,0:T(8,128)} %param.10) | copy-start | bytes 15748
  2.1 17.9 %all-to-all-start = ((f32[32,4,512]{2,1,0:T(4,128)}), f32[32,4,512]{2,1,0:T(4,128)S(1)}, u32[]{:S(2)}, u32[]{:S(2)}) async-start(f32[32,4,512]{2,1,0:T(4,128)} %broadcast_in_dim.13), calls=%async_computation | async-start | bytes 524288 | tf_op jit(solution)/shard_map/all_to_all | solution.py:217
  9.4 0.7 %copy-start.2 = (f32[3]{0:T(128)S(1)}, f32[3]{0:T(128)}, u32[]{:S(2)}) copy-start(f32[3]{0:T(128)} %param.8) | copy-start | bytes 40

commit v4 on v3

--- a/solution.py
+++ b/solution.py
@@ -23,7 +23,7 @@
     return jnp.broadcast_to(ref[pl.ds(row, 1), :], (SUBLANES, LANES))
 
 
-def kernel(all_ref, slot_ref, table_ref, scalars, white_ref, part_ref,
+def kernel(same_ref, other_ref, slot_ref, table_ref, scalars, white_ref, part_ref,
            slots, far_index, far_rows, singles, doubles, final, scaled, inverses):
     owners, capacity = table_ref.shape
     count, local = slot_ref.shape
@@ -44,16 +44,22 @@
 
     far_index[...] = jnp.zeros(far_index.shape, jnp.int32)
     far_index[:, :capacity] = table_ref[...]
-    for base in range(0, owners, SUBLANES):
-        index = far_index[base : base + SUBLANES, :]
+    parity = device % 2
+    for first, ref, base in [
+        (start, ref, base)
+        for start, ref in ((parity, same_ref), (1 - parity, other_ref))
+        for base in range(0, owners // 2, SUBLANES)
+    ]:
+        theirs = pl.ds(first + 2 * base, SUBLANES, stride=2)
+        index = far_index[theirs, :]
         lane, chunk = index & (LANES - 1), index >> 7
         for c in range(CHANNELS):
             value = None
             for g in range(groups):
-                source = all_ref[pl.ds(base * rows_each + g * CHANNELS + c, SUBLANES, stride=rows_each), :]
+                source = ref[pl.ds(base * rows_each + g * CHANNELS + c, SUBLANES, stride=rows_each), :]
                 picked = lane_gather(source, lane)
                 value = picked if value is None else jnp.where(chunk == g, picked, value)
-            far_rows[c, base : base + SUBLANES, :] = value
+            far_rows[c, theirs, :] = value
 
     slots[count:, :] = jnp.zeros((slots.shape[0] - count, local), jnp.int32)
     slots[:count, :] = slot_ref[...]
@@ -72,9 +78,9 @@
         place = place - capacity
 
     neighbours = [
-        jnp.maximum(tile_id - 1, 0) * n_slabs + slab_id,
-        device,
-        jnp.minimum(tile_id + 1, n_tiles - 1) * n_slabs + slab_id,
+        (jnp.maximum(tile_id - 1, 0) * n_slabs + slab_id) // 2,
+        device // 2,
+        (jnp.minimum(tile_id + 1, n_tiles - 1) * n_slabs + slab_id) // 2,
     ]
 
     def gather(p, g):
@@ -86,7 +92,7 @@
             for q in range(groups):
                 here = chunk == t * groups + q
                 for c in range(CHANNELS):
-                    picked = lane_gather(tile_of(all_ref, neighbours[t] * rows_each + q * CHANNELS + c), lane)
+                    picked = lane_gather(tile_of(same_ref, neighbours[t] * rows_each + q * CHANNELS + c), lane)
                     found[c] = picked if found[c] is None else jnp.where(here, picked, found[c])
         if g == 0:
             distant = mine >= near_slots
@@ -103,7 +109,7 @@
                 doubles[c, pl.ds(start, SUBLANES, stride=SUBLANES), :] = value
         if p == panels - 1 and g == groups - 1:
             for c in range(CHANNELS):
-                own = all_ref[pl.ds(device * rows_each + c, groups, stride=CHANNELS), :]
+                own = same_ref[pl.ds(device // 2 * rows_each + c, groups, stride=CHANNELS), :]
                 if c < 3:
                     own = own * scales[c][:groups]
                     singles[c, count * groups : (count + 1) * groups, :] = own
@@ -213,9 +219,18 @@
     assert capacity <= LANES and panels * EARLY <= LANES
     devices = lax.axis_size("pts") * lax.axis_size("grp")
     payload = jnp.concatenate([coords, observations[None, :]], axis=0)
-    everything = jnp.broadcast_to(payload[None], (devices, CHANNELS, local))
-    everything = lax.all_to_all(everything, AXES, split_axis=0, concat_axis=0, tiled=True)
-    everything = everything.reshape(devices, CHANNELS, groups, LANES).transpose(0, 2, 1, 3)
+    n_slabs = lax.axis_size("grp")
+    assert n_slabs % 2 == 0 and devices % (2 * SUBLANES) == 0
+    alike = [[d for d in range(devices) if d % 2 == parity] for parity in range(2)]
+    same = jnp.broadcast_to(payload[None], (devices // 2, CHANNELS, local))
+    same = lax.all_to_all(same, AXES, split_axis=0, concat_axis=0, tiled=True, axis_index_groups=alike)
+    same, length_scales, nugget = lax.optimization_barrier((same, length_scales, nugget))
+    other = lax.ppermute(same, "grp", [(i, i ^ 1) for i in range(n_slabs)])
+
+    def rows(received):
+        received = received.reshape(devices // 2, CHANNELS, groups, LANES).transpose(0, 2, 1, 3)
+        return received.reshape(devices // 2 * CHANNELS * groups, LANES)
+
     scalars = jnp.concatenate([length_scales, nugget])[None]
     vmem = pl.BlockSpec(memory_space=pltpu.VMEM)
     white, part = pl.pallas_call(
@@ -224,7 +239,7 @@
             jax.ShapeDtypeStruct((groups, LANES), jnp.float32),
             jax.ShapeDtypeStruct((devices, LANES), jnp.float32),
         ),
-        in_specs=[vmem, vmem, vmem, vmem],
+        in_specs=[vmem] * 5,
         out_specs=(vmem, vmem),
         scratch_shapes=[
             pltpu.VMEM((panels * SUBLANES, local), jnp.int32),
@@ -237,7 +252,7 @@
             pltpu.VMEM((order * SUBLANES, LANES), jnp.float32),
         ],
         compiler_params=pltpu.CompilerParams(vmem_limit_bytes=16 << 20),
-    )(everything.reshape(devices * CHANNELS * groups, LANES), slot_of, fetch_table[0], scalars)
+    )(rows(same), rows(other), slot_of, fetch_table[0], scalars)
     parts = lax.all_to_all(part, AXES, split_axis=0, concat_axis=0, tiled=True)
     neg_loglik = jnp.sum(parts) / (2.0 * local * devices) + half_log_tau
     return (white.reshape(local), neg_loglik)

time: 35.4 us -> 33.7 us (0.952)
  blocking collectives: 9.37 us -> 24.9 us
  waiting for transfers between devices: 9.82 us -> 0.6 us
  starting transfers between devices: 7.33 us -> 0.01 us
  local copies, waits for them, and re-layouts: 0.74 us -> 0.04 us
    all_to_all x0 -> x1, blocking collectives: none -> 16.1 us  [body(): lax.all_to_all(same, AXES, split_axis=0, concat_axis=0, tiled=True, axis_...]
    all_to_all x1 -> x0, waiting for transfers between devices: 9.82 us -> none  [body(): lax.all_to_all(everything, AXES, split_axis=0, concat_axis=0, tiled=True)]
    all_to_all x1 -> x0, starting transfers between devices: 7.33 us -> none  [body(): lax.all_to_all(everything, AXES, split_axis=0, concat_axis=0, tiled=True)]
    broadcast_in_dim x1, local copies, waits for them, and re-layouts: 0.73 us -> 0.02 us  [body(): same = jnp.broadcast_to(payload[None], (devices // 2, CHANNELS, local))]
    ppermute x0 -> x1, waiting for transfers between devices: none -> 0.6 us  [body(): other = lax.ppermute(same, 'grp', [(i, i ^ 1) for i in range(n_slabs)])]
    all_to_all x1, blocking collectives: 9.37 us -> 8.85 us  [body(): parts = lax.all_to_all(part, AXES, split_axis=0, concat_axis=0, tiled=True)]
where the time goes in v4:
time: 33.7 us; the launch traced here: 33.4 us
  blocking collectives  24.9 us (74%)
  Pallas kernels  3.26 us (10%)
  between operations  3.1 us (9%)
  other arithmetic  1.43 us (4%)
  waiting for transfers between devices  0.6 us (2%)
    all_to_all x1, blocking collectives, body(): lax.all_to_all(same, AXES, split_axis=0, concat_axis=0, tiled=True, axis_...  16.1 us
    all_to_all x1, blocking collectives, body(): parts = lax.all_to_all(part, AXES, split_axis=0, concat_axis=0, tiled=True)  8.85 us
    pallas_call x1, Pallas kernels, body(): pl.pallas_call(kernel, out_shape=(jax.ShapeDtypeStruct((groups, LANES), j...  3.26 us
    concatenate x1, other arithmetic, body(): payload = jnp.concatenate([coords, observations[None, :]], axis=0)  0.72 us
  transfers between devices with their start and end apart: 1, of which 1 were waited for; matrix products, arithmetic and copies ran while one was open for 0% of the time, Pallas kernels for 0%

profile of v4, /device:TPU:0, one launch (start us, length us, event | category | flops | bytes accessed | tf_op | source)
XLA Modules:
  0.0 33.4 jit_solution(14578714278728885472)
XLA Ops:
  0.6 0.7 %pad_maximum_fusion = f32[4,512]{1,0:T(4,128)S(1)} fusion(f32[1,512]{1,0:T(1,128)} %bitcast.22, f32[3,512]{1,0:T(4,128)} %param.6), kind=kLoop, calls=%fused_computation | loop fusion | flops 2048 | bytes 16384 | tf_op jit(solution)/shard_map/concatenate | solution.py:221
  1.4 0.0 copy-start
  1.4 0.0 copy-start.1
  1.4 16.1 %all_to_all.14 = f32[16,4,512]{2,1,0:T(4,128)S(1)} all-to-all(f32[16,4,512]{2,1,0:T(4,128)S(1)} %broadcast_in_dim.13), channel_id=1, replica_groups={{0,2,4,6,8,10,12,14,16,18,20,22,24,26,28,30},{1,3,5,7,9,11,13,15,17,19,..., dimensions={0} | all-to-all | bytes 262144 | tf_op jit(solution)/shard_map/all_to_all | solution.py:226
  17.5 0.0 copy-start.2
  17.5 0.0 collective-permute-start
  18.1 0.0 copy-done.2
  18.1 0.1 maximum_bitcast_fusion.scalars
  18.2 0.6 %collective-permute-done = f32[16,4,512]{2,1,0:T(4,128)S(1)} collective-permute-done((f32[16,4,512]{2,1,0:T(4,128)S(1)}, f32[16,4,512]{2,1,0:T(4,128)S(1)}, u32[]{:S(2)}, u32[]{:S(2)}) %collective-permute-start) | collective-permute-done | bytes 131104 | tf_op jit(solution)/shard_map/ppermute | solution.py:228
  18.8 0.0 copy-done
  18.8 0.0 copy-done.1
  18.8 3.3 %shard_map.77 = (f32[4,128]{1,0:T(4,128)}, f32[32,128]{1,0:T(8,128)S(1)}) custom-call(f32[256,128]{1,0:T(8,128)S(1)} %bitcast.18, f32[256,128]{1,0:T(8,128)S(1)} %bitcast.19, s32[30,512]{1,0:T(8,128)S(1)} %copy-done, s32[32,41]{1,0:T(8,128)S(1)} %bitcast.21, f32[1,4]{1,0:T(1,128)S(1)} %maximum_bitcast_fusion.scalars), custom_call_target="tpu_custom_call" | custom-call | tf_op jit(solution)/shard_map/pallas_call | solution.py:236
  22.1 8.9 %all_to_all.15 = f32[32,1,128]{2,1,0:T(1,128)S(1)} all-to-all(f32[32,1,128]{2,1,0:T(1,128)S(1)} %bitcast.20), channel_id=1, replica_groups=mesh['pts'=8,'grp'=4] {'pts','grp'}, dimensions={0} | all-to-all | bytes 32768 | tf_op jit(solution)/shard_map/all_to_all | solution.py:256
  30.9 0.6 %reduce_sum.9 = f32[]{:T(128)} reduce(f32[32,1,128]{2,1,0:T(1,128)S(1)} %all_to_all.15, f32[]{:T(128)} %constant.1.clone.1), dimensions={0,1,2}, to_apply=%region_0.0 | reduce | flops 4095 | bytes 16392 | tf_op jit(solution)/shard_map/reduce_sum | solution.py:257
  (1 shorter events, 0.0 us)
Async XLA Ops:
  1.4 17.4 %copy-start = (s32[30,512]{1,0:T(8,128)S(1)}, s32[30,512]{1,0:T(8,128)}, u32[]{:S(2)}) copy-start(s32[30,512]{1,0:T(8,128)} %slot_ref.1) | copy-start | bytes 184324
  1.4 17.4 %copy-start.1 = (s32[1,32,41]{2,1,0:T(8,128)S(1)}, s32[1,32,41]{2,1,0:T(8,128)}, u32[]{:S(2)}) copy-start(s32[1,32,41]{2,1,0:T(8,128)} %param.10) | copy-start | bytes 15748
  17.5 0.7 %copy-start.2 = (f32[3]{0:T(128)S(1)}, f32[3]{0:T(128)}, u32[]{:S(2)}) copy-start(f32[3]{0:T(128)} %param.8) | copy-start | bytes 40
  17.5 1.3 %collective-permute-start = (f32[16,4,512]{2,1,0:T(4,128)S(1)}, f32[16,4,512]{2,1,0:T(4,128)S(1)}, u32[]{:S(2)}, u32[]{:S(2)}) collective-permute-start(f32[16,4,512]{2,1,0:T(4,128)S(1)} %all_to_all.14), channel_id=1, source_target_pairs={{0,1},{1,0},{2,3},{3,2},{4,5},{5,4},{6,7},{7,6},{8,9},{9,8},{10,11... | collective-permute-start | bytes 393224 | tf_op jit(solution)/shard_map/ppermute | solution.py:228

commit v5 on v4

--- a/solution.py
+++ b/solution.py
@@ -207,6 +207,13 @@
         eliminate(p, [(p + 1, g) for g in range(groups)] if p + 1 < panels else [])
 
 
+def finish(parts_ref, white_ref, out_ref, total_ref):
+    out_ref[...] = white_ref[...]
+    points = parts_ref.shape[0] * white_ref.shape[0] * white_ref.shape[1]
+    total = jnp.sum(jnp.sum(parts_ref[...], axis=0, keepdims=True), axis=1, keepdims=True)
+    total_ref[...] = total / (2.0 * points) + half_log_tau
+
+
 def body(coords, observations, length_scales, nugget, fetch_table, slot_of):
     local = coords.shape[1]
     owners, capacity = fetch_table.shape[1:]
@@ -254,8 +261,17 @@
         compiler_params=pltpu.CompilerParams(vmem_limit_bytes=16 << 20),
     )(rows(same), rows(other), slot_of, fetch_table[0], scalars)
     parts = lax.all_to_all(part, AXES, split_axis=0, concat_axis=0, tiled=True)
-    neg_loglik = jnp.sum(parts) / (2.0 * local * devices) + half_log_tau
-    return (white.reshape(local), neg_loglik)
+    white, neg_loglik = pl.pallas_call(
+        finish,
+        out_shape=(
+            jax.ShapeDtypeStruct((groups, LANES), jnp.float32),
+            jax.ShapeDtypeStruct((1, 1), jnp.float32),
+        ),
+        in_specs=[vmem, vmem],
+        out_specs=(vmem, vmem),
+        compiler_params=pltpu.CompilerParams(vmem_limit_bytes=1 << 20),
+    )(parts, white)
+    return (white.reshape(local), neg_loglik[0, 0])
 
 
 def solution(mesh):

time: 33.7 us -> 31.3 us (0.929)
  between operations: 3.1 us -> 1.33 us
  other arithmetic: 1.43 us -> 0.8 us
    reduce_sum x1 -> x0, other arithmetic: 0.63 us -> none  [body(): neg_loglik = jnp.sum(parts) / (2.0 * local * devices) + half_log_tau]
    pallas_call x0 -> x1, Pallas kernels: none -> 0.6 us  [body(): pl.pallas_call(finish, out_shape=(jax.ShapeDtypeStruct((groups, LANES), j...]
    pallas_call x1, Pallas kernels: 3.26 us -> 2.68 us  [body(): pl.pallas_call(kernel, out_shape=(jax.ShapeDtypeStruct((groups, LANES), j...]
where the time goes in v5:
time: 31.3 us; the launch traced here: 31 us
  blocking collectives  24.9 us (80%)
  Pallas kernels  3.28 us (10%)
  between operations  1.33 us (4%)
  other arithmetic  0.8 us (3%)
  waiting for transfers between devices  0.6 us (2%)
    all_to_all x1, blocking collectives, body(): lax.all_to_all(same, AXES, split_axis=0, concat_axis=0, tiled=True, axis_...  16.1 us
    all_to_all x1, blocking collectives, body(): parts = lax.all_to_all(part, AXES, split_axis=0, concat_axis=0, tiled=True)  8.87 us
    pallas_call x1, Pallas kernels, body(): pl.pallas_call(kernel, out_shape=(jax.ShapeDtypeStruct((groups, LANES), j...  2.68 us
    concatenate x1, other arithmetic, body(): payload = jnp.concatenate([coords, observations[None, :]], axis=0)  0.72 us
  transfers between devices with their start and end apart: 1, of which 1 were waited for; matrix products, arithmetic and copies ran while one was open for 0% of the time, Pallas kernels for 0%

profile of v5, /device:TPU:0, one launch (start us, length us, event | category | flops | bytes accessed | tf_op | source)
XLA Modules:
  0.0 31.0 jit_solution(7386171830779512751)
XLA Ops:
  0.6 0.7 %pad_maximum_fusion = f32[4,512]{1,0:T(4,128)S(1)} fusion(f32[1,512]{1,0:T(1,128)} %bitcast.25, f32[3,512]{1,0:T(4,128)} %param.6), kind=kLoop, calls=%fused_computation | loop fusion | flops 2048 | bytes 16384 | tf_op jit(solution)/shard_map/concatenate | solution.py:228
  1.4 0.0 copy-start
  1.4 0.0 copy-start.1
  1.4 16.1 %all_to_all.16 = f32[16,4,512]{2,1,0:T(4,128)S(1)} all-to-all(f32[16,4,512]{2,1,0:T(4,128)S(1)} %broadcast_in_dim.13), channel_id=1, replica_groups={{0,2,4,6,8,10,12,14,16,18,20,22,24,26,28,30},{1,3,5,7,9,11,13,15,17,19,..., dimensions={0} | all-to-all | bytes 262144 | tf_op jit(solution)/shard_map/all_to_all | solution.py:233
  17.5 0.0 copy-start.2
  17.5 0.0 collective-permute-start
  18.1 0.0 copy-done.2
  18.1 0.1 maximum_bitcast_fusion.scalars
  18.2 0.6 %collective-permute-done = f32[16,4,512]{2,1,0:T(4,128)S(1)} collective-permute-done((f32[16,4,512]{2,1,0:T(4,128)S(1)}, f32[16,4,512]{2,1,0:T(4,128)S(1)}, u32[]{:S(2)}, u32[]{:S(2)}) %collective-permute-start) | collective-permute-done | bytes 131104 | tf_op jit(solution)/shard_map/ppermute | solution.py:235
  18.8 0.0 copy-done
  18.8 0.0 copy-done.1
  18.8 2.7 %shard_map.77 = (f32[4,128]{1,0:T(4,128)S(1)}, f32[32,128]{1,0:T(8,128)S(1)}) custom-call(f32[256,128]{1,0:T(8,128)S(1)} %bitcast.20, f32[256,128]{1,0:T(8,128)S(1)} %bitcast.21, s32[30,512]{1,0:T(8,128)S(1)} %copy-done, s32[32,41]{1,0:T(8,128)S(1)} %bitcast.24, f32[1,4]{1,0:T(1,128)S(1)} %maximum_bitcast_fusion.scalars), custom_call_target="tpu_custom_call" | custom-call | tf_op jit(solution)/shard_map/pallas_call | solution.py:243
  21.5 8.9 %all_to_all.17 = f32[32,1,128]{2,1,0:T(1,128)S(1)} all-to-all(f32[32,1,128]{2,1,0:T(1,128)S(1)} %bitcast.23), channel_id=1, replica_groups=mesh['pts'=8,'grp'=4] {'pts','grp'}, dimensions={0} | all-to-all | bytes 32768 | tf_op jit(solution)/shard_map/all_to_all | solution.py:263
  30.4 0.6 %shard_map.78 = (f32[4,128]{1,0:T(4,128)}, f32[1,1]{1,0:T(1,128)}) custom-call(f32[32,128]{1,0:T(8,128)S(1)} %bitcast.22, f32[4,128]{1,0:T(4,128)S(1)} %get-tuple-element.13.white_ref), custom_call_target="tpu_custom_call" | custom-call | tf_op jit(solution)/shard_map/pallas_call | solution.py:264
  (1 shorter events, 0.0 us)
Async XLA Ops:
  1.4 17.4 %copy-start = (s32[30,512]{1,0:T(8,128)S(1)}, s32[30,512]{1,0:T(8,128)}, u32[]{:S(2)}) copy-start(s32[30,512]{1,0:T(8,128)} %slot_ref.1) | copy-start | bytes 184324
  1.4 17.4 %copy-start.1 = (s32[1,32,41]{2,1,0:T(8,128)S(1)}, s32[1,32,41]{2,1,0:T(8,128)}, u32[]{:S(2)}) copy-start(s32[1,32,41]{2,1,0:T(8,128)} %param.10) | copy-start | bytes 15748
  17.5 0.7 %copy-start.2 = (f32[3]{0:T(128)S(1)}, f32[3]{0:T(128)}, u32[]{:S(2)}) copy-start(f32[3]{0:T(128)} %param.8) | copy-start | bytes 40
  17.5 1.3 %collective-permute-start = (f32[16,4,512]{2,1,0:T(4,128)S(1)}, f32[16,4,512]{2,1,0:T(4,128)S(1)}, u32[]{:S(2)}, u32[]{:S(2)}) collective-permute-start(f32[16,4,512]{2,1,0:T(4,128)S(1)} %all_to_all.16), channel_id=1, source_target_pairs={{0,1},{1,0},{2,3},{3,2},{4,5},{5,4},{6,7},{7,6},{8,9},{9,8},{10,11... | collective-permute-start | bytes 393224 | tf_op jit(solution)/shard_map/ppermute | solution.py:235

commit v6 on v5

--- a/solution.py
+++ b/solution.py
@@ -45,13 +45,12 @@
     far_index[...] = jnp.zeros(far_index.shape, jnp.int32)
     far_index[:, :capacity] = table_ref[...]
     parity = device % 2
-    for first, ref, base in [
-        (start, ref, base)
-        for start, ref in ((parity, same_ref), (1 - parity, other_ref))
+    for start, first, ref, base in [
+        (start, first, ref, base)
+        for start, first, ref in ((0, parity, same_ref), (owners // 2, 1 - parity, other_ref))
         for base in range(0, owners // 2, SUBLANES)
     ]:
-        theirs = pl.ds(first + 2 * base, SUBLANES, stride=2)
-        index = far_index[theirs, :]
+        index = far_index[pl.ds(first + 2 * base, SUBLANES, stride=2), :]
         lane, chunk = index & (LANES - 1), index >> 7
         for c in range(CHANNELS):
             value = None
@@ -59,7 +58,7 @@
                 source = ref[pl.ds(base * rows_each + g * CHANNELS + c, SUBLANES, stride=rows_each), :]
                 picked = lane_gather(source, lane)
                 value = picked if value is None else jnp.where(chunk == g, picked, value)
-            far_rows[c, theirs, :] = value
+            far_rows[c, start + base : start + base + SUBLANES, :] = value
 
     slots[count:, :] = jnp.zeros((slots.shape[0] - count, local), jnp.int32)
     slots[:count, :] = slot_ref[...]
@@ -68,14 +67,15 @@
     for p in range(1, panels):
         moved = pltpu.roll(slots[p * SUBLANES : (p + 1) * SUBLANES, :LANES], p * EARLY, 1)
         packed = jnp.where(lane_id < p * EARLY, packed, moved)
-    place = packed - near_slots
     far = [jnp.zeros(full, jnp.float32)] * CHANNELS
     for o in range(owners):
+        if o % (owners // 2) == 0:
+            place = packed - near_slots - capacity * (parity if o == 0 else 1 - parity)
         here = (place >= 0) & (place < capacity)
         lane = place & (LANES - 1)
         for c in range(CHANNELS):
             far[c] = jnp.where(here, lane_gather(tile_of(far_rows.at[c], o), lane), far[c])
-        place = place - capacity
+        place = place - 2 * capacity
 
     neighbours = [
         (jnp.maximum(tile_id - 1, 0) * n_slabs + slab_id) // 2,

time: 31.3 us -> 31.3 us (level)
  no operation moved by 1% of the time
where the time goes in v6:
time: 31.3 us; the launch traced here: 31 us
  blocking collectives  24.9 us (80%)
  Pallas kernels  3.28 us (10%)
  between operations  1.33 us (4%)
  other arithmetic  0.8 us (3%)
  waiting for transfers between devices  0.6 us (2%)
    all_to_all x1, blocking collectives, body(): lax.all_to_all(same, AXES, split_axis=0, concat_axis=0, tiled=True, axis_...  16.1 us
    all_to_all x1, blocking collectives, body(): parts = lax.all_to_all(part, AXES, split_axis=0, concat_axis=0, tiled=True)  8.87 us
    pallas_call x1, Pallas kernels, body(): pl.pallas_call(kernel, out_shape=(jax.ShapeDtypeStruct((groups, LANES), j...  2.68 us
    concatenate x1, other arithmetic, body(): payload = jnp.concatenate([coords, observations[None, :]], axis=0)  0.72 us
  transfers between devices with their start and end apart: 1, of which 1 were waited for; matrix products, arithmetic and copies ran while one was open for 0% of the time, Pallas kernels for 0%

profile of v6, /device:TPU:0, one launch (start us, length us, event | category | flops | bytes accessed | tf_op | source)
XLA Modules:
  0.0 31.0 jit_solution(13282813191921224902)
XLA Ops:
  0.6 0.7 %pad_maximum_fusion = f32[4,512]{1,0:T(4,128)S(1)} fusion(f32[1,512]{1,0:T(1,128)} %bitcast.25, f32[3,512]{1,0:T(4,128)} %param.6), kind=kLoop, calls=%fused_computation | loop fusion | flops 2048 | bytes 16384 | tf_op jit(solution)/shard_map/concatenate | solution.py:228
  1.4 0.0 copy-start
  1.4 0.0 copy-start.1
  1.4 16.1 %all_to_all.16 = f32[16,4,512]{2,1,0:T(4,128)S(1)} all-to-all(f32[16,4,512]{2,1,0:T(4,128)S(1)} %broadcast_in_dim.13), channel_id=1, replica_groups={{0,2,4,6,8,10,12,14,16,18,20,22,24,26,28,30},{1,3,5,7,9,11,13,15,17,19,..., dimensions={0} | all-to-all | bytes 262144 | tf_op jit(solution)/shard_map/all_to_all | solution.py:233
  17.5 0.0 copy-start.2
  17.5 0.0 collective-permute-start
  18.1 0.0 copy-done.2
  18.1 0.1 maximum_bitcast_fusion.scalars
  18.2 0.6 %collective-permute-done = f32[16,4,512]{2,1,0:T(4,128)S(1)} collective-permute-done((f32[16,4,512]{2,1,0:T(4,128)S(1)}, f32[16,4,512]{2,1,0:T(4,128)S(1)}, u32[]{:S(2)}, u32[]{:S(2)}) %collective-permute-start) | collective-permute-done | bytes 131104 | tf_op jit(solution)/shard_map/ppermute | solution.py:235
  18.8 0.0 copy-done
  18.8 0.0 copy-done.1
  18.8 2.7 %shard_map.77 = (f32[4,128]{1,0:T(4,128)S(1)}, f32[32,128]{1,0:T(8,128)S(1)}) custom-call(f32[256,128]{1,0:T(8,128)S(1)} %bitcast.20, f32[256,128]{1,0:T(8,128)S(1)} %bitcast.21, s32[30,512]{1,0:T(8,128)S(1)} %copy-done, s32[32,41]{1,0:T(8,128)S(1)} %bitcast.24, f32[1,4]{1,0:T(1,128)S(1)} %maximum_bitcast_fusion.scalars), custom_call_target="tpu_custom_call" | custom-call | tf_op jit(solution)/shard_map/pallas_call | solution.py:243
  21.5 8.9 %all_to_all.17 = f32[32,1,128]{2,1,0:T(1,128)S(1)} all-to-all(f32[32,1,128]{2,1,0:T(1,128)S(1)} %bitcast.23), channel_id=1, replica_groups=mesh['pts'=8,'grp'=4] {'pts','grp'}, dimensions={0} | all-to-all | bytes 32768 | tf_op jit(solution)/shard_map/all_to_all | solution.py:263
  30.4 0.6 %shard_map.78 = (f32[4,128]{1,0:T(4,128)}, f32[1,1]{1,0:T(1,128)}) custom-call(f32[32,128]{1,0:T(8,128)S(1)} %bitcast.22, f32[4,128]{1,0:T(4,128)S(1)} %get-tuple-element.13.white_ref), custom_call_target="tpu_custom_call" | custom-call | tf_op jit(solution)/shard_map/pallas_call | solution.py:264
  (1 shorter events, 0.0 us)
Async XLA Ops:
  1.4 17.4 %copy-start = (s32[30,512]{1,0:T(8,128)S(1)}, s32[30,512]{1,0:T(8,128)}, u32[]{:S(2)}) copy-start(s32[30,512]{1,0:T(8,128)} %slot_ref.1) | copy-start | bytes 184324
  1.4 17.4 %copy-start.1 = (s32[1,32,41]{2,1,0:T(8,128)S(1)}, s32[1,32,41]{2,1,0:T(8,128)}, u32[]{:S(2)}) copy-start(s32[1,32,41]{2,1,0:T(8,128)} %param.10) | copy-start | bytes 15748
  17.5 0.7 %copy-start.2 = (f32[3]{0:T(128)S(1)}, f32[3]{0:T(128)}, u32[]{:S(2)}) copy-start(f32[3]{0:T(128)} %param.8) | copy-start | bytes 40
  17.5 1.3 %collective-permute-start = (f32[16,4,512]{2,1,0:T(4,128)S(1)}, f32[16,4,512]{2,1,0:T(4,128)S(1)}, u32[]{:S(2)}, u32[]{:S(2)}) collective-permute-start(f32[16,4,512]{2,1,0:T(4,128)S(1)} %all_to_all.16), channel_id=1, source_target_pairs={{0,1},{1,0},{2,3},{3,2},{4,5},{5,4},{6,7},{7,6},{8,9},{9,8},{10,11... | collective-permute-start | bytes 393224 | tf_op jit(solution)/shard_map/ppermute | solution.py:235
